TPU v7x, 128 devices: a whole 4x4x4 slice. The times are simulated.
128 devices in a mesh: req: 16 (over x, z), tp: 8 (over y, core).
Axes of the slice: x: 4, y: 4, z: 4, core: 2. Of those that a mesh axis runs over, the one named last changes fastest.
Arguments:
- hidden: bfloat16 [8192, 2048], P('req', 'tp'), may hold values from -6 to 6
- qkv_weight: bfloat16 [2048, 3072], P('req', 'tp'), may hold values from -0.125 to 0.125
- out_weight: bfloat16 [2048, 2048], P('tp', 'req'), may hold values from -0.125 to 0.125
- kv_pages: bfloat16 [1024, 128, 1024], P('req', None, 'tp'), may hold values from -160 to 160, as said below
- cache_pages: int32 [16], replicated, may hold values from 1 to 256, 960 in all
- slot_order: int32 [1024], replicated, may hold values from 0 to 1023, each once
Outputs:
- attention_out: bfloat16 [8192, 2048], P('req', 'tp')
- pages_out: bfloat16 [1024, 128, 1024], P('req', None, 'tp')
Inputs may be any that keep to these rules, and one draw needn't show every extreme that they name: `cache_pages`: each request has at least one cached page and at most 256, and one request has exactly 256; all cached pages plus 4 new pages per request fill exactly 1024 slots. `slot_order`: each global slot appears once. `kv_pages`: cached rotated keys and values.
All inputs are finite; a program needn't handle non-finite values.
Results may differ from a plain program's by a relative error of at most 0.02.
The roundings to bfloat16 on the way count: a program that leaves them out, or rounds other values in their place, can miss the bound.
Values may be sent and summed in bfloat16 or wider, within the bound.
A program may use at most 128 MiB of HBM per device.

v0:
```python
import math
import jax
import jax.numpy as jnp
from jax import lax
from jax.sharding import PartitionSpec as P

HD = 64
GROUP = 4
SPAN = 512
THETA = 1000000.0
NEG_BIG = -1e30


def rotary(values, positions):
    head_width = values.shape[-1]
    half_width = head_width // 2
    inv_freq = jnp.power(THETA, -(jnp.arange(half_width, dtype=jnp.float32) * 2.0 / head_width))
    angles = positions.astype(jnp.float32)[..., None] * inv_freq
    cosines = jnp.cos(angles)
    sines = jnp.sin(angles)
    lower_half = values[..., :half_width]
    upper_half = values[..., half_width:]
    return jnp.concatenate(
        [lower_half * cosines - upper_half * sines, upper_half * cosines + lower_half * sines],
        axis=-1,
    )


def to_columns(stat):
    return jnp.moveaxis(stat, -1, -3)[..., None]


def locate(slot_ids, cache_pages, slot_order, new_pages):
    requests = cache_pages.shape[0]
    slot_count = slot_order.shape[0]
    counts = cache_pages + new_pages
    page_ends = jnp.cumsum(counts)
    starts = page_ends - counts
    ranking = jnp.sum(
        jnp.where(
            slot_order[None, :] == slot_ids[:, None],
            jnp.arange(slot_count, dtype=jnp.int32)[None, :],
            0,
        ),
        axis=1,
    )
    holder = jnp.sum((starts[None, :] <= ranking[:, None]).astype(jnp.int32), axis=1) - 1
    onehot = jnp.arange(requests, dtype=jnp.int32)[None, :] == holder[:, None]
    first_page = jnp.sum(jnp.where(onehot, starts[None, :], 0), axis=1)
    cached = jnp.sum(jnp.where(onehot, cache_pages[None, :], 0), axis=1)
    return (holder, ranking - first_page, cached)


def write_pages(kv_pages, fresh, slot_req, page_index, cached, new_pages):
    page_rows = kv_pages.shape[1]
    lane_width = kv_pages.shape[2]
    fresh_pages = fresh.reshape(-1, page_rows, lane_width)
    pick = slot_req * new_pages + jnp.clip(page_index - cached, 0, new_pages - 1)
    return jnp.where((page_index >= cached)[:, None, None], fresh_pages[pick], kv_pages)


def block_terms(queries, query_start, page_block, slot_req, key_start, is_live):
    block_slots = page_block.shape[0]
    page_rows = page_block.shape[1]
    kv_heads = queries.shape[2]
    head_width = queries.shape[4]
    span_rows = queries.shape[1]
    kv_pairs = page_block.reshape(block_slots, page_rows, kv_heads, 2, head_width)
    key_rows = kv_pairs[:, :, :, 0, :]
    value_rows = kv_pairs[:, :, :, 1, :]
    chosen = queries[slot_req]
    scores = jnp.einsum(
        "bckgd,bpkd->bkgcp", chosen, key_rows, preferred_element_type=jnp.float32
    ) * (1.0 / math.sqrt(head_width))
    query_pos = query_start[slot_req][:, None] + jnp.arange(span_rows, dtype=jnp.int32)[None, :]
    key_pos = key_start[:, None] + jnp.arange(page_rows, dtype=jnp.int32)[None, :]
    visible = (key_pos[:, None, :] <= query_pos[:, :, None]) & is_live[:, None, None]
    visible = visible[:, None, None, :, :]
    masked = jnp.where(visible, scores, NEG_BIG)
    block_max = jnp.max(masked, axis=-1)
    exp_terms = jnp.where(visible, jnp.exp(masked - block_max[..., None]), 0.0)
    block_sum = jnp.sum(exp_terms, axis=-1)
    weights = exp_terms.astype(jnp.bfloat16)
    block_out = jnp.einsum(
        "bkgcp,bpkd->bckgd", weights, value_rows, preferred_element_type=jnp.float32
    )
    return (block_out, block_max, block_sum)


def fold(running, terms, slot_req):
    acc_out, acc_max, acc_sum = running
    block_out, block_max, block_sum = terms
    for j in range(block_out.shape[0]):
        target = slot_req[j]
        old_max = lax.dynamic_index_in_dim(acc_max, target, 0, keepdims=False)
        new_max = jnp.maximum(old_max, block_max[j])
        keep_old = jnp.exp(old_max - new_max)
        take_new = jnp.exp(block_max[j] - new_max)
        old_out = lax.dynamic_index_in_dim(acc_out, target, 0, keepdims=False)
        old_sum = lax.dynamic_index_in_dim(acc_sum, target, 0, keepdims=False)
        acc_out = lax.dynamic_update_index_in_dim(
            acc_out, old_out * to_columns(keep_old) + block_out[j] * to_columns(take_new), target, 0
        )
        acc_sum = lax.dynamic_update_index_in_dim(
            acc_sum, old_sum * keep_old + block_sum[j] * take_new, target, 0
        )
        acc_max = lax.dynamic_update_index_in_dim(acc_max, new_max, target, 0)
    return (acc_out, acc_max, acc_sum)


def init_state(requests, span_rows, kv_heads, group_size, head_width):
    return (
        jnp.zeros((requests, span_rows, kv_heads, group_size, head_width), jnp.float32),
        jnp.full((requests, kv_heads, group_size, span_rows), NEG_BIG, jnp.float32),
        jnp.zeros((requests, kv_heads, group_size, span_rows), jnp.float32),
    )


def body(hidden, qkv_weight, out_weight, kv_pages, cache_pages, slot_order):
    whole = lax.all_gather(hidden, "tp", axis=1, tiled=True)
    tok_rows = whole.shape[0]
    projected = jnp.dot(
        whole,
        lax.all_gather(qkv_weight, "req", axis=0, tiled=True),
        preferred_element_type=jnp.float32,
    )
    local_slots = kv_pages.shape[0]
    page_rows = kv_pages.shape[1]
    lane_width = kv_pages.shape[2]
    kv_heads = lane_width // (2 * HD)
    local_reqs = tok_rows // SPAN
    new_pages = SPAN // page_rows
    my_index = lax.axis_index("req")
    query_start = cache_pages * page_rows
    home_start = lax.dynamic_slice_in_dim(query_start, my_index * local_reqs, local_reqs, 0)
    projected = projected.reshape(local_reqs, SPAN, kv_heads, GROUP + 2, HD)
    positions = (home_start[:, None] + jnp.arange(SPAN, dtype=jnp.int32)[None, :])[:, :, None, None]
    queries = rotary(projected[:, :, :, :GROUP, :], positions).astype(jnp.bfloat16)
    key_new = rotary(projected[:, :, :, GROUP : GROUP + 1, :], positions).astype(jnp.bfloat16)
    value_new = projected[:, :, :, GROUP + 1 :, :].astype(jnp.bfloat16)
    fresh = jnp.concatenate([key_new, value_new], axis=3).reshape(local_reqs, SPAN, lane_width)
    my_slots = my_index * local_slots + jnp.arange(local_slots, dtype=jnp.int32)
    block_slots = math.gcd(local_slots, max(1, 512 // page_rows))
    fresh_all = lax.all_gather(fresh, "req", axis=0, tiled=True)
    slot_req, page_index, cached = locate(my_slots, cache_pages, slot_order, new_pages)
    pages_out = write_pages(kv_pages, fresh_all, slot_req, page_index, cached, new_pages)
    piece_pages = lax.all_gather(pages_out, "req", axis=0, tiled=True)
    piece_count = piece_pages.shape[0]
    piece_ids = jnp.arange(piece_count, dtype=jnp.int32)
    piece_req, piece_index, unused_cached = locate(piece_ids, cache_pages, slot_order, new_pages)
    local_req = piece_req - my_index * local_reqs
    is_mine = (local_req >= 0) & (local_req < local_reqs)
    ordering = jnp.argsort(jnp.where(is_mine, 0, 1).astype(jnp.int32), stable=True)
    ordering = jnp.concatenate([ordering, jnp.zeros((block_slots,), jnp.int32)])
    used_count = jnp.sum(is_mine.astype(jnp.int32))

    def advance(j, state_now):
        low_slot = j * block_slots
        picked = lax.dynamic_slice_in_dim(ordering, low_slot, block_slots, 0)
        page_block = piece_pages[picked]
        is_live = low_slot + jnp.arange(block_slots, dtype=jnp.int32) < used_count
        block_req = jnp.clip(local_req[picked], 0, local_reqs - 1)
        key_start = piece_index[picked] * page_rows
        terms = block_terms(queries, home_start, page_block, block_req, key_start, is_live)
        return fold(state_now, terms, block_req)

    acc_out, acc_max, acc_sum = lax.fori_loop(
        0,
        (used_count + block_slots - 1) // block_slots,
        advance,
        init_state(local_reqs, SPAN, kv_heads, GROUP, HD),
    )
    attention = acc_out / to_columns(acc_sum)
    attention_flat = attention.astype(jnp.bfloat16).reshape(tok_rows, kv_heads * GROUP * HD)
    head_terms = jnp.dot(
        attention_flat,
        lax.all_gather(out_weight, "req", axis=1, tiled=True),
        preferred_element_type=jnp.float32,
    )
    attention_out = lax.psum_scatter(
        head_terms.astype(jnp.bfloat16), "tp", scatter_dimension=1, tiled=True
    )
    return (attention_out, pages_out)


def solution(mesh):
    return jax.shard_map(
        body,
        mesh=mesh,
        in_specs=(P("req", "tp"), P("req", "tp"), P("tp", "req"), P("req", None, "tp"), P(), P()),
        out_specs=(P("req", "tp"), P("req", None, "tp")),
        check_vma=False,
    )
```

profile of v0, /device:TPU:0, one launch (start us, length us, event | category | flops | bytes accessed | tf_op | source)
XLA Modules:
  0.0 880.7 jit_solution(123321950454702308)
XLA Ops:
  11.6 45.0 %all-gather.8.cloned.1.call-done = bf16[2048,384]{1,0:T(8,128)(2,1)} async-done(((bf16[128,384]{1,0:T(8,128)(2,1)}), bf16[2048,384]{1,0:T(8,128)(2,1)}) %all-gather.8.cloned.1.call-update) | async-done | bytes 1572880 | tf_op jit(solution)/shard_map/all_gather | solution.py:124
  56.5 27.8 %all-gather.6.cloned.1.call-done = bf16[512,2048]{1,0:T(8,128)(2,1)} async-done(((bf16[512,256]{1,0:T(8,128)(2,1)}), bf16[512,2048]{1,0:T(8,128)(2,1)}) %all-gather.6.cloned.1.call-update) | async-done | bytes 2097168 | tf_op jit(solution)/shard_map/all_gather | solution.py:120
  84.3 3.1 fusion.54
  89.0 45.6 %all-gather.10.cloned.1.call-done = bf16[16,512,128]{2,1,0:T(8,128)(2,1)} async-done(((bf16[1,512,128]{2,1,0:T(8,128)(2,1)}), bf16[16,512,128]{2,1,0:T(8,128)(2,1)}) %all-gather.10.cloned.1.call-update) | async-done | bytes 2097168 | tf_op jit(solution)/shard_map/all_gather | solution.py:144
  134.6 2.5 gather_fusion.2
  137.1 3.2 broadcast_select_fusion
  143.2 4.4 sort.17
  147.8 189.2 %all-gather.12.cloned.1.call-done = bf16[1024,128,128]{2,1,0:T(8,128)(2,1)} async-done(((bf16[64,128,128]{2,1,0:T(8,128)(2,1)}), bf16[1024,128,128]{2,1,0:T(8,128)(2,1)}) %all-gather.12.cloned.1.call-update) | async-done | bytes 33554448 | tf_op jit(solution)/shard_map/all_gather | solution.py:147
  337.1 130.7 %while.15 = (s32[]{:T(128)}, f32[1,512,1,4,64]{1,4,3,0,2:T(8,128)S(1)}, f32[1,1,4,512]{3,2,1,0:T(4,128)S(1)}, f32[1,1,4,512]{3,2,1,0:T(4,128)S(1)}, s32[]{:T(128...) while((s32[]{:T(128)}, ...), condition=%wide.region_13.14_spmd.clone, body=%wide.region_10.13_spmd.clone.sunk | while | flops 284227616 | bytes 20279676 | solution.py:167
  339.4 1.4 gather_fusion.1
  347.0 1.4 gather_fusion.1
  354.7 1.4 gather_fusion.1
  362.4 1.4 gather_fusion.1
  370.1 1.4 gather_fusion.1
  377.8 1.4 gather_fusion.1
  385.5 1.4 gather_fusion.1
  393.2 1.4 gather_fusion.1
  400.8 1.4 gather_fusion.1
  408.5 1.4 gather_fusion.1
  416.2 1.4 gather_fusion.1
  423.9 1.4 gather_fusion.1
  431.6 1.4 gather_fusion.1
  467.8 3.3 convolution_convert_fusion
  471.2 402.6 %reduce-scatter.2.cloned.1.call-done = bf16[512,256]{1,0:T(8,128)(2,1)} async-done(((bf16[512,2048]{1,0:T(8,128)(2,1)}), bf16[512,256]{1,0:T(8,128)(2,1)}) %reduce-scatter.2.cloned.1.call-update) | async-done | bytes 262160 | tf_op jit(solution)/shard_map/reduce_scatter | solution.py:180
  (328 shorter events, 120.1 us)
Async XLA Ops:
  7.2 81.7 %copy-start.1 = (s32[16]{0:T(128)S(1)}, s32[16]{0:T(128)}, u32[]{:S(2)}) copy-start(s32[16]{0:T(128)} %param.12) | copy-start | bytes 196
  7.2 81.4 %copy-start = (s32[1024]{0:T(1024)S(1)}, s32[1024]{0:T(1024)}, u32[]{:S(2)}) copy-start(s32[1024]{0:T(1024)} %param.13) | copy-start | bytes 12292
  7.2 49.3 %all-gather.8.cloned.1.call-start = ((), (), s32[]{:S(2)}) async-start(), calls=%async_computation.2 | async-start | bytes 1671168 | tf_op jit(solution)/shard_map/all_gather | solution.py:124
  7.9 76.4 %all-gather.6.cloned.1.call-start = ((), (), s32[]{:S(2)}) async-start(), calls=%async_computation.1 | async-start | bytes 2359296 | tf_op jit(solution)/shard_map/all_gather | solution.py:120
  8.7 125.9 %all-gather.10.cloned.1.call-start = ((), (), s32[]{:S(2)}) async-start(), calls=%async_computation.3 | async-start | bytes 2228224 | tf_op jit(solution)/shard_map/all_gather | solution.py:144
  88.5 248.5 %all-gather.12.cloned.1.call-start = ((), (), s32[]{:S(2)}) async-start(), calls=%async_computation.4 | async-start | bytes 35651584 | tf_op jit(solution)/shard_map/all_gather | solution.py:147
  140.4 327.4 %all-gather.14.cloned.1.call-start = ((), (), s32[]{:S(2)}) async-start(), calls=%async_computation.5 | async-start | bytes 1114112 | tf_op jit(solution)/shard_map/all_gather | solution.py:177
  141.0 732.8 %reduce-scatter.2.cloned.1.call-start = ((), (), s32[]{:S(2)}) async-start(), calls=%async_computation.6 | async-start | bytes 2359296 | tf_op jit(solution)/shard_map/reduce_scatter | solution.py:180
Sparse Core Ops, SparseCore 0:
  10.2 46.2 all-gather.7
  58.2 26.0 all-gather.5
  88.6 45.9 all-gather.9
  140.5 196.4 all-gather.11
  338.9 42.8 all-gather.13
  471.3 402.4 reduce-scatter.1
where the time goes:
time: 887 us; the launch traced here: 881 us
  waiting for transfers between devices  712 us (80%)
  other arithmetic  68.7 us (8%)
  matrix products  43.1 us (5%)
  local copies, waits for them, and re-layouts  40.3 us (5%)
  between operations  14.9 us (2%)
    reduce_scatter x1, waiting for transfers between devices, body(): lax.psum_scatter(head_terms.astype(jnp.bfloat16), 'tp', scatter_dimension...  403 us
    all_gather x1, waiting for transfers between devices, body(): piece_pages = lax.all_gather(pages_out, 'req', axis=0, tiled=True)  189 us
    all_gather x1, waiting for transfers between devices, body(): fresh_all = lax.all_gather(fresh, 'req', axis=0, tiled=True)  45.6 us
    all_gather x1, waiting for transfers between devices, body(): lax.all_gather(qkv_weight, 'req', axis=0, tiled=True)  45 us
    all_gather x1, waiting for transfers between devices, body(): whole = lax.all_gather(hidden, 'tp', axis=1, tiled=True)  27.8 us
    gather x34, local copies, waits for them, and re-layouts, advance(): page_block = piece_pages[picked]  25.6 us
    dot_general x17, matrix products, block_terms(): jnp.einsum('bkgcp,bpkd->bckgd', weights, value_rows, preferred_element_ty...  21.1 us
    reduce_sum x17, other arithmetic, block_terms(): block_sum = jnp.sum(exp_terms, axis=-1)  18.6 us
  transfers between devices with their start and end apart: 6, of which 5 were waited for; matrix products, arithmetic and copies ran while one was open for 16% of the time, Pallas kernels for 0%

commit v1 on v0

--- a/solution.py
+++ b/solution.py
@@ -9,6 +9,12 @@
 SPAN = 512
 THETA = 1000000.0
 NEG_BIG = -1e30
+
+
+def gather_from_all(x, axis, dim):
+    peers = lax.axis_size(axis)
+    repeats = [peers if d == dim else 1 for d in range(x.ndim)]
+    return lax.all_to_all(jnp.tile(x, repeats), axis, split_axis=dim, concat_axis=dim, tiled=True)
 
 
 def rotary(values, positions):
@@ -120,9 +126,7 @@
     whole = lax.all_gather(hidden, "tp", axis=1, tiled=True)
     tok_rows = whole.shape[0]
     projected = jnp.dot(
-        whole,
-        lax.all_gather(qkv_weight, "req", axis=0, tiled=True),
-        preferred_element_type=jnp.float32,
+        whole, gather_from_all(qkv_weight, "req", 0), preferred_element_type=jnp.float32
     )
     local_slots = kv_pages.shape[0]
     page_rows = kv_pages.shape[1]

time: 887 us -> 844 us (0.952)
  waiting for transfers between devices: 712 us -> 659 us
    all_gather x1 -> x0, waiting for transfers between devices: 45 us -> none  [body(): lax.all_gather(qkv_weight, 'req', axis=0, tiled=True)]
    all_gather x1, waiting for transfers between devices: 27.8 us -> 0.02 us  [body(): whole = lax.all_gather(hidden, 'tp', axis=1, tiled=True)]
    all_to_all x0 -> x1, waiting for transfers between devices: none -> 22.2 us  [gather_from_all(): lax.all_to_all(jnp.tile(x, repeats), axis, split_axis=dim, concat_axis=di...]
  transfers between devices with their start and end apart: 6 -> 6, of which waited for: 5 -> 4; matrix products, arithmetic and copies ran while one was open for 16% -> 17% of each run, Pallas kernels for 0% -> 0%
where the time goes in v1:
time: 844 us; the launch traced here: 837 us
  waiting for transfers between devices  659 us (78%)
  other arithmetic  67.2 us (8%)
  local copies, waits for them, and re-layouts  44.4 us (5%)
  matrix products  42.8 us (5%)
  between operations  14.6 us (2%)
    reduce_scatter x1, waiting for transfers between devices, body(): lax.psum_scatter(head_terms.astype(jnp.bfloat16), 'tp', scatter_dimension...  403 us
    all_gather x1, waiting for transfers between devices, body(): piece_pages = lax.all_gather(pages_out, 'req', axis=0, tiled=True)  189 us
    all_gather x1, waiting for transfers between devices, body(): fresh_all = lax.all_gather(fresh, 'req', axis=0, tiled=True)  43.1 us
    gather x34, local copies, waits for them, and re-layouts, advance(): page_block = piece_pages[picked]  25.5 us
    all_to_all x1, waiting for transfers between devices, gather_from_all(): lax.all_to_all(jnp.tile(x, repeats), axis, split_axis=dim, concat_axis=di...  22.2 us
    dot_general x17, matrix products, block_terms(): jnp.einsum('bkgcp,bpkd->bckgd', weights, value_rows, preferred_element_ty...  20.9 us
    reduce_sum x17, other arithmetic, block_terms(): block_sum = jnp.sum(exp_terms, axis=-1)  18.5 us
  transfers between devices with their start and end apart: 6, of which 4 were waited for; matrix products, arithmetic and copies ran while one was open for 17% of the time, Pallas kernels for 0%

profile of v1, /device:TPU:0, one launch (start us, length us, event | category | flops | bytes accessed | tf_op | source)
XLA Modules:
  0.0 837.4 jit_solution(10830407321671779915)
XLA Ops:
  8.9 1.4 tile.2
  10.4 8.0 all-to-all-start
  20.0 22.2 %all-to-all-done = bf16[16,128,384]{1,2,0:T(8,128)(2,1)S(1)} async-done(((bf16[16,128,384]{1,2,0:T(8,128)(2,1)}), bf16[16,128,384]{1,2,0:T(8,128)(2,1)S(1)}, u32[]{:S(2)}, u32[]{:S(2)}) %all-to-all-start) | async-done | bytes 1572896 | tf_op jit(solution)/shard_map/all_to_all | solution.py:17
  43.8 2.6 fusion.47
  48.1 43.1 %all-gather.7.cloned.1.call-done = bf16[16,512,128]{2,1,0:T(8,128)(2,1)} async-done(((bf16[1,512,128]{2,1,0:T(8,128)(2,1)}), bf16[16,512,128]{2,1,0:T(8,128)(2,1)}) %all-gather.7.cloned.1.call-update) | async-done | bytes 2097168 | tf_op jit(solution)/shard_map/all_gather | solution.py:148
  91.1 2.5 gather_fusion.2
  93.7 3.2 broadcast_select_fusion
  99.7 4.4 sort.17
  104.3 189.2 %all-gather.9.cloned.1.call-done = bf16[1024,128,128]{2,1,0:T(8,128)(2,1)} async-done(((bf16[64,128,128]{2,1,0:T(8,128)(2,1)}), bf16[1024,128,128]{2,1,0:T(8,128)(2,1)}) %all-gather.9.cloned.1.call-update) | async-done | bytes 33554448 | tf_op jit(solution)/shard_map/all_gather | solution.py:151
  293.6 130.7 %while.15 = (s32[]{:T(128)}, f32[1,512,1,4,64]{1,4,3,0,2:T(8,128)S(1)}, f32[1,1,4,512]{3,2,1,0:T(4,128)S(1)}, f32[1,1,4,512]{3,2,1,0:T(4,128)S(1)}, s32[]{:T(128...) while((s32[]{:T(128)}, ...), condition=%wide.region_13.14_spmd.clone, body=%wide.region_10.13_spmd.clone.sunk | while | flops 284227616 | bytes 20279676 | solution.py:171
  295.9 1.4 gather_fusion.1
  303.6 1.4 gather_fusion.1
  311.2 1.4 gather_fusion.1
  318.9 1.4 gather_fusion.1
  326.6 1.4 gather_fusion.1
  334.3 1.4 gather_fusion.1
  342.0 1.4 gather_fusion.1
  349.7 1.4 gather_fusion.1
  357.4 1.4 gather_fusion.1
  365.1 1.4 gather_fusion.1
  372.8 1.4 gather_fusion.1
  380.4 1.4 gather_fusion.1
  424.4 3.3 convolution_convert_fusion
  427.7 403.1 %reduce-scatter.2.cloned.1.call-done = bf16[512,256]{1,0:T(8,128)(2,1)} async-done(((bf16[512,2048]{1,0:T(8,128)(2,1)}), bf16[512,256]{1,0:T(8,128)(2,1)}) %reduce-scatter.2.cloned.1.call-update) | async-done | bytes 262160 | tf_op jit(solution)/shard_map/reduce_scatter | solution.py:184
  (331 shorter events, 122.0 us)
Async XLA Ops:
  7.2 11.3 %copy-start.1 = (s32[16]{0:T(128)S(1)}, s32[16]{0:T(128)}, u32[]{:S(2)}) copy-start(s32[16]{0:T(128)} %param.12) | copy-start | bytes 196
  7.2 36.6 %all-gather.5.cloned.1.call-start = ((), (), s32[]{:S(2)}) async-start(), calls=%async_computation.2 | async-start | bytes 2359296 | tf_op jit(solution)/shard_map/all_gather | solution.py:126
  10.4 31.8 %all-to-all-start = ((bf16[16,128,384]{1,2,0:T(8,128)(2,1)}), bf16[16,128,384]{1,2,0:T(8,128)(2,1)S(1)}, u32[]{:S(2)}, u32[]{:S(2)}) async-start(bf16[16,128,384]{1,2,0:T(8,128)(2,1)} %tile.2), calls=%async_computation | async-start | bytes 3145728 | tf_op jit(solution)/shard_map/all_to_all | solution.py:17
  18.4 72.8 %all-gather.7.cloned.1.call-start = ((), (), s32[]{:S(2)}) async-start(), calls=%async_computation.3 | async-start | bytes 2228224 | tf_op jit(solution)/shard_map/all_gather | solution.py:148
  43.8 3.8 copy-start
  47.6 245.9 %all-gather.9.cloned.1.call-start = ((), (), s32[]{:S(2)}) async-start(), calls=%async_computation.4 | async-start | bytes 35651584 | tf_op jit(solution)/shard_map/all_gather | solution.py:151
  96.9 327.5 %all-gather.11.cloned.1.call-start = ((), (), s32[]{:S(2)}) async-start(), calls=%async_computation.5 | async-start | bytes 1114112 | tf_op jit(solution)/shard_map/all_gather | solution.py:181
  97.5 733.4 %reduce-scatter.2.cloned.1.call-start = ((), (), s32[]{:S(2)}) async-start(), calls=%async_computation.6 | async-start | bytes 2359296 | tf_op jit(solution)/shard_map/reduce_scatter | solution.py:184
Sparse Core Ops, SparseCore 0:
  9.7 29.2 all-gather.4
  47.7 43.3 all-gather.6
  97.0 196.4 all-gather.8
  295.5 42.8 all-gather.10
  427.9 402.9 reduce-scatter.1
